TPU v7x, 256 devices: a whole 4x4x8 slice. The times are simulated.
256 devices in a mesh: particle: 16 (over y, z_hi), coeffici: 8 (over x, core), half: 2 (over z_lo).
Axes of the slice: x: 4, y: 4, z: 8 (z_hi: 4, z_lo: 2; z = z_hi * 2 + z_lo), core: 2. Of those that a mesh axis runs over, the one named last changes fastest.
Arguments:
- residuals: float32 [2, 16384, 16384], P('half', 'particle', 'coeffici'), may hold values from -6 to 6
- loadings: float32 [2, 16384, 256], P('half', 'coeffici'), may hold values from -0.046875 to 0.046875
Outputs:
- new_loadings: float32 [2, 16384, 256], P('half', ('coeffici', 'particle'))
- rayleigh: float32 [2, 256, 256], P('half')
All inputs are finite; a program needn't handle non-finite values.
Results may differ from a plain program's by a relative error of at most 0.00024.
Values sent between devices are 32-bit elements; how exact they have to be, the bound alone decides.
No kernel may reach another device: no remote copies, remote signals or barrier semaphores. Data moves between devices by JAX's collectives and lax.ppermute only.
A program may use at most 64 MiB of HBM per device.

v0:
```python
import math
import jax
import jax.numpy as jnp
from jax import lax
from jax.sharding import PartitionSpec as P


def from_partner(value, axis, distance):
    mask = 2**distance
    pairs = [(source, source ^ mask) for source in range(lax.axis_size(axis))]
    return lax.ppermute(value, axis, pairs)


def contract_rows(left, right):
    return lax.dot_general(
        left,
        right,
        (((0,), (0,)), ((), ())),
        precision=lax.Precision.HIGHEST,
        preferred_element_type=jnp.float32,
    )


def local(residuals, loadings):
    samples = residuals[0]
    loading = loadings[0]
    factor = 1.0 / math.sqrt(samples.shape[0] * lax.axis_size("particle"))
    partial_value = jnp.dot(
        samples, loading, precision=lax.Precision.HIGHEST, preferred_element_type=jnp.float32
    )
    scores = lax.psum(partial_value, "coeffici")
    share_rows = samples.shape[1] // lax.axis_size("particle")
    first_row = lax.axis_index("particle") * share_rows
    local_cov = contract_rows(samples, scores)
    covariance = lax.psum(local_cov, "particle") * factor
    partner = from_partner(covariance, "half", 0)
    shrunk = covariance * jax.nn.sigmoid(covariance * partner)
    correlation = contract_rows(loading, shrunk)
    rayleigh = lax.psum(correlation, "coeffici") * factor
    weighted = lax.dynamic_slice_in_dim(shrunk, first_row, share_rows, 0)
    return (weighted[None], rayleigh[None])


def solution(mesh):
    in_specs = (P("half", "particle", "coeffici"), P("half", "coeffici", None))
    out_specs = (P("half", ("coeffici", "particle"), None), P("half", None, None))
    return jax.shard_map(local, mesh=mesh, in_specs=in_specs, out_specs=out_specs, check_vma=False)
```

profile of v0, /device:TPU:8, one launch (start us, length us, event | category | flops | bytes accessed | tf_op | source)
XLA Modules:
  0.0 395.9 jit_solution(12921856936748713425)
XLA Ops:
  7.2 0.0 copy-start
  7.2 0.0 all-reduce.4.cloned.1.call-start
  7.2 1.5 copy-done
  8.8 9.9 %fusion.2 = f32[1024,256]{1,0:T(8,128)} fusion(f32[1,1024,2048]{2,1,0:T(8,128)} %param.2, f32[1,2048,256]{2,1,0:T(8,128)S(1)} %copy-done), kind=kOutput, calls=%fused_computation.2 | convolution fusion | flops 6442450944 | bytes 11534336 | tf_op jit(solution)/shard_map/dot_general | solution.py:28
  18.6 0.0 all-reduce.4.cloned.1.call-update
  18.7 0.0 all-reduce.6.cloned.1.call-start
  18.7 70.6 %all-reduce.4.cloned.1.call-done = f32[1024,256]{1,0:T(8,128)} async-done(((f32[1024,256]{1,0:T(8,128)}), f32[1024,256]{1,0:T(8,128)}) %all-reduce.4.cloned.1.call-update) | async-done | bytes 1048592 | tf_op jit(solution)/shard_map/psum | solution.py:31
  89.3 10.7 %fusion.4 = f32[2048,256]{0,1:T(8,128)} fusion(f32[1024,256]{1,0:T(8,128)} %all-reduce.4.cloned.1.call-done, f32[1,1024,2048]{2,1,0:T(8,128)} %param.2), kind=kOutput, calls=%fused_computation.4 | convolution fusion | flops 6442450944 | bytes 11534336 | tf_op jit(solution)/shard_map/dot_general | solution.py:15
  100.1 0.0 all-reduce.6.cloned.1.call-update
  100.1 0.0 all-reduce.8.cloned.1.call-start
  100.1 175.1 %all-reduce.6.cloned.1.call-done = f32[2048,256]{0,1:T(8,128)} async-done(((f32[2048,256]{0,1:T(8,128)}), f32[2048,256]{0,1:T(8,128)}) %all-reduce.6.cloned.1.call-update) | async-done | bytes 2097168 | tf_op jit(solution)/shard_map/psum | solution.py:35
  275.3 1.9 broadcast_multiply_fusion
  277.2 2.2 collective-permute-start
  279.3 38.0 %collective-permute-done = f32[2048,256]{0,1:T(8,128)S(1)} collective-permute-done((f32[2048,256]{0,1:T(8,128)S(1)}, f32[2048,256]{0,1:T(8,128)S(1)}, u32[]{:S(2)}, u32[]{:S(2)}) %collective-permute-start) | collective-permute-done | bytes 2097184 | tf_op jit(solution)/shard_map/ppermute | solution.py:11
  317.3 0.0 copy-done.2
  317.3 0.9 divide_multiply_fusion
  318.3 1.3 copy-done.1
  319.6 2.6 fusion.10
  322.2 0.0 all-reduce.8.cloned.1.call-update
  322.2 0.9 constant_dynamic-slice_fusion
  323.2 0.8 copy.5
  323.9 63.6 %all-reduce.8.cloned.1.call-done = f32[256,256]{0,1:T(8,128)} async-done(((f32[256,256]{0,1:T(8,128)}), f32[256,256]{0,1:T(8,128)}) %all-reduce.8.cloned.1.call-update) | async-done | bytes 262160 | tf_op jit(solution)/shard_map/psum | solution.py:39
  387.5 1.0 multiply_bitcast_fusion
  388.5 0.8 copy.6
  (2 shorter events, 0.0 us)
Async XLA Ops:
  7.2 1.6 copy-start
  7.2 82.2 %all-reduce.4.cloned.1.call-start = ((), (), s32[]{:S(2)}) async-start(), calls=%async_computation | async-start | bytes 2097152 | tf_op jit(solution)/shard_map/psum | solution.py:31
  18.7 256.6 %all-reduce.6.cloned.1.call-start = ((), (), s32[]{:S(2)}) async-start(), calls=%async_computation.1 | async-start | bytes 4194304 | tf_op jit(solution)/shard_map/psum | solution.py:35
  100.1 287.4 %all-reduce.8.cloned.1.call-start = ((), (), s32[]{:S(2)}) async-start(), calls=%async_computation.2 | async-start | bytes 524288 | tf_op jit(solution)/shard_map/psum | solution.py:39
  275.3 42.1 %copy-start.2 = (f32[2048,256]{0,1:T(8,128)S(1)}, f32[2048,256]{0,1:T(8,128)}, u32[]{:S(2)}) copy-start(f32[2048,256]{0,1:T(8,128)} %all-reduce.6.cloned.1.call-done) | copy-start | bytes 6291460
  277.2 40.2 %collective-permute-start = (f32[2048,256]{0,1:T(8,128)S(1)}, f32[2048,256]{0,1:T(8,128)S(1)}, u32[]{:S(2)}, u32[]{:S(2)}) collective-permute-start(f32[2048,256]{0,1:T(8,128)S(1)} %broadcast_multiply_fusion), channel_id=1, source_target_pairs={{0,1},{1,0},{2,3},{3,2},{4,5},{5,4},{6,7},{7,6},{8,9},{9,8},{10,11... | collective-permute-start | bytes 6291464 | tf_op jit(solution)/shard_map/ppermute | solution.py:11
  318.3 1.3 copy-start.1
Sparse Core Ops, SparseCore 0:
  18.8 70.5 all-reduce.3
  100.2 175.0 all-reduce.5
  322.3 65.1 all-reduce.7
where the time goes:
time: 396 us
  waiting for transfers between devices  347 us (88%)
  matrix products  23.2 us (6%)
  between operations  13.8 us (3%)
  local copies, waits for them, and re-layouts  5.38 us (1%)
    psum x1, waiting for transfers between devices, local(): covariance = lax.psum(local_cov, 'particle') * factor  175 us
    psum x1, waiting for transfers between devices, local(): scores = lax.psum(partial_value, 'coeffici')  70.6 us
    psum x1, waiting for transfers between devices, local(): rayleigh = lax.psum(correlation, 'coeffici') * factor  63.6 us
    ppermute x1, waiting for transfers between devices, from_partner(): return lax.ppermute(value, axis, pairs)  38 us
    dot_general x2, matrix products, contract_rows(): lax.dot_general(left, right, (((0,), (0,)), ((), ())), precision=lax.Prec...  13.3 us
    dot_general x1, matrix products, local(): jnp.dot(samples, loading, precision=lax.Precision.HIGHEST, preferred_elem...  9.87 us
  transfers between devices with their start and end apart: 4, of which 4 were waited for; matrix products, arithmetic and copies ran while one was open for 0% of the time, Pallas kernels for 0%

commit v1 on v0

--- a/solution.py
+++ b/solution.py
@@ -32,7 +32,7 @@
     share_rows = samples.shape[1] // lax.axis_size("particle")
     first_row = lax.axis_index("particle") * share_rows
     local_cov = contract_rows(samples, scores)
-    covariance = lax.psum(local_cov, "particle") * factor
+    covariance = jnp.sum(lax.all_gather(local_cov, "particle"), axis=0) * factor
     partner = from_partner(covariance, "half", 0)
     shrunk = covariance * jax.nn.sigmoid(covariance * partner)
     correlation = contract_rows(loading, shrunk)

time: 396 us -> 635 us (1.60)
  waiting for transfers between devices: 347 us -> 553 us
  local copies, waits for them, and re-layouts: 5.38 us -> 34.1 us
  other arithmetic: 3.78 us -> 10.2 us
    all_gather x0 -> x1, waiting for transfers between devices: none -> 373 us  [local(): covariance = jnp.sum(lax.all_gather(local_cov, 'particle'), axis=0) * factor]
    psum x1 -> x0, waiting for transfers between devices: 175 us -> none  [local(): covariance = lax.psum(local_cov, 'particle') * factor]
    unnamed x7 -> x6, local copies, waits for them, and re-layouts: 3.7 us -> 32.5 us
    ppermute x1, waiting for transfers between devices: 38 us -> 47.2 us  [from_partner(): return lax.ppermute(value, axis, pairs)]
    reduce_sum x0 -> x1, other arithmetic: none -> 8.14 us  [local(): covariance = jnp.sum(lax.all_gather(local_cov, 'particle'), axis=0) * factor]
where the time goes in v1:
time: 635 us
  waiting for transfers between devices  553 us (87%)
  local copies, waits for them, and re-layouts  34.1 us (5%)
  matrix products  23.2 us (4%)
  between operations  13.8 us (2%)
  other arithmetic  10.2 us (2%)
    all_gather x1, waiting for transfers between devices, local(): covariance = jnp.sum(lax.all_gather(local_cov, 'particle'), axis=0) * factor  373 us
    psum x1, waiting for transfers between devices, local(): scores = lax.psum(partial_value, 'coeffici')  70.7 us
    psum x1, waiting for transfers between devices, local(): rayleigh = lax.psum(correlation, 'coeffici') * factor  62.2 us
    ppermute x1, waiting for transfers between devices, from_partner(): return lax.ppermute(value, axis, pairs)  47.2 us
    unnamed x6, local copies, waits for them, and re-layouts  32.5 us
    dot_general x2, matrix products, contract_rows(): lax.dot_general(left, right, (((0,), (0,)), ((), ())), precision=lax.Prec...  13.3 us
  transfers between devices with their start and end apart: 4, of which 4 were waited for; matrix products, arithmetic and copies ran while one was open for 0% of the time, Pallas kernels for 0%

profile of v1, /device:TPU:8, one launch (start us, length us, event | category | flops | bytes accessed | tf_op | source)
XLA Modules:
  0.0 634.6 jit_solution(10022962787195907429)
XLA Ops:
  7.2 0.0 all-reduce.3.cloned.1.call-start
  7.2 1.5 copy-done
  8.8 9.9 %fusion.2 = f32[1024,256]{1,0:T(8,128)} fusion(f32[1,1024,2048]{2,1,0:T(8,128)} %param.2, f32[1,2048,256]{2,1,0:T(8,128)S(1)} %copy-done), kind=kOutput, calls=%fused_computation.3 | convolution fusion | flops 6442450944 | bytes 11534336 | tf_op jit(solution)/shard_map/dot_general | solution.py:28
  18.6 0.0 all-reduce.3.cloned.1.call-update
  18.7 0.0 all-gather.3.cloned.1.call-start
  18.7 70.7 %all-reduce.3.cloned.1.call-done = f32[1024,256]{1,0:T(8,128)} async-done(((f32[1024,256]{1,0:T(8,128)}), f32[1024,256]{1,0:T(8,128)}) %all-reduce.3.cloned.1.call-update) | async-done | bytes 1048592 | tf_op jit(solution)/shard_map/psum | solution.py:31
  89.4 10.7 %fusion.4 = f32[2048,256]{0,1:T(8,128)} fusion(f32[1024,256]{1,0:T(8,128)} %all-reduce.3.cloned.1.call-done, f32[1,1024,2048]{2,1,0:T(8,128)} %param.2), kind=kOutput, calls=%fused_computation.5 | convolution fusion | flops 6442450944 | bytes 11534336 | tf_op jit(solution)/shard_map/dot_general | solution.py:15
  100.1 0.0 all-gather.3.cloned.1.call-update
  100.2 0.2 all-reduce.5.cloned.1.call-start
  100.4 372.7 %all-gather.3.cloned.1.call-done = f32[32768,256]{0,1:T(8,128)} async-done(((f32[2048,256]{0,1:T(8,128)}), f32[32768,256]{0,1:T(8,128)}) %all-gather.3.cloned.1.call-update) | async-done | bytes 33554448 | tf_op jit(solution)/shard_map/all_gather | solution.py:35
  473.1 28.8 %copy.8 = f32[32,8,16,2048]{3,2,1,0:T(8,128)S(1)} copy(f32[32,8,16,2048]{3,1,2,0:T(8,128)} %bitcast.28) | data formatting | bytes 67108864
  501.9 8.1 %bitcast_reduce_fusion = f32[2048,256]{0,1:T(8,128)S(1)} fusion(f32[32,8,16,2048]{3,2,1,0:T(8,128)S(1)} %copy.8), kind=kLoop, calls=%fused_computation | loop fusion | flops 7864320 | bytes 35651584 | tf_op jit(solution)/shard_map/reduce_sum | solution.py:35
  510.0 0.2 broadcast_multiply_fusion
  510.2 0.1 collective-permute-start
  510.3 47.2 %collective-permute-done = f32[2048,256]{0,1:T(8,128)S(1)} collective-permute-done((f32[2048,256]{0,1:T(8,128)S(1)}, f32[2048,256]{0,1:T(8,128)S(1)}, u32[]{:S(2)}, u32[]{:S(2)}) %collective-permute-start) | collective-permute-done | bytes 2097184 | tf_op jit(solution)/shard_map/ppermute | solution.py:11
  557.5 0.9 divide_multiply_fusion
  558.4 1.3 copy-done.1
  559.7 2.6 fusion.10
  562.4 0.0 all-reduce.5.cloned.1.call-update
  562.4 0.9 constant_dynamic-slice_fusion
  563.3 0.8 copy.6
  564.1 62.2 %all-reduce.5.cloned.1.call-done = f32[256,256]{0,1:T(8,128)} async-done(((f32[256,256]{0,1:T(8,128)}), f32[256,256]{0,1:T(8,128)}) %all-reduce.5.cloned.1.call-update) | async-done | bytes 262160 | tf_op jit(solution)/shard_map/psum | solution.py:39
  626.3 1.0 multiply_bitcast_fusion
  627.3 0.8 copy.7
  (2 shorter events, 0.0 us)
Async XLA Ops:
  7.2 1.6 copy-start
  7.2 82.3 %all-reduce.3.cloned.1.call-start = ((), (), s32[]{:S(2)}) async-start(), calls=%async_computation | async-start | bytes 2097152 | tf_op jit(solution)/shard_map/psum | solution.py:31
  18.7 454.5 %all-gather.3.cloned.1.call-start = ((), (), s32[]{:S(2)}) async-start(), calls=%async_computation.2 | async-start | bytes 35651584 | tf_op jit(solution)/shard_map/all_gather | solution.py:35
  100.2 526.1 %all-reduce.5.cloned.1.call-start = ((), (), s32[]{:S(2)}) async-start(), calls=%async_computation.1 | async-start | bytes 524288 | tf_op jit(solution)/shard_map/psum | solution.py:39
  510.2 47.3 %collective-permute-start = (f32[2048,256]{0,1:T(8,128)S(1)}, f32[2048,256]{0,1:T(8,128)S(1)}, u32[]{:S(2)}, u32[]{:S(2)}) collective-permute-start(f32[2048,256]{0,1:T(8,128)S(1)} %broadcast_multiply_fusion), channel_id=1, source_target_pairs={{0,1},{1,0},{2,3},{3,2},{4,5},{5,4},{6,7},{7,6},{8,9},{9,8},{10,11... | collective-permute-start | bytes 6291464 | tf_op jit(solution)/shard_map/ppermute | solution.py:11
  558.4 1.3 copy-start.1
Sparse Core Ops, SparseCore 0:
  18.8 70.6 all-reduce.2
  100.3 372.7 all-gather.2
  562.5 63.7 all-reduce.4
